TPU v7x, 128 devices: a whole 4x4x4 slice. The times are simulated.
128 devices in a mesh: row: 16 (over z, y_hi, core), col: 8 (over y_lo, x).
Axes of the slice: x: 4, y: 4 (y_hi: 2, y_lo: 2; y = y_hi * 2 + y_lo), z: 4, core: 2. Of those that a mesh axis runs over, the one named last changes fastest.
Arguments:
- packed_tiles: bfloat16 [768, 128, 1024], P('row', None, 'col'), may hold values from -6 to 6
- source_pick: int32 [16, 48], P('row'), may hold values from 0 to 47, each once within a row
- owner_place: int32 [16, 48], P('row'), may hold values from 0 to 47, each once within a row
- tile_orient: int32 [16, 48], P('row'), may hold values from 0 to 3
- w_panel: bfloat16 [4096, 12288], P('row', 'col'), may hold values from -0.09375 to 0.09375
Outputs:
- particle_hole: bfloat16 [24576, 12288], P('row', 'col')
Inputs may be any that keep to these rules, and one draw needn't show every extreme that they name: `source_pick`: each row is a permutation of the stored tiles' local indices. `owner_place`: each row is a permutation of the received items.
All inputs are finite; a program needn't handle non-finite values.
Results may differ from a plain program's by a relative error of at most 0.001.
Values may be sent and summed in bfloat16 or wider, within the bound.
No kernel may reach another device: no remote copies, remote signals or barrier semaphores. Data moves between devices by JAX's collectives and lax.ppermute only.
A program may use at most 128 MiB of HBM per device.

v0:
```python
import jax
import jax.numpy as jnp
from jax import lax
from jax.sharding import PartitionSpec as P

VW = 768
KC = 512


def orient_tiles(tile_set, orient_codes):
    flipped = (jnp.remainder(orient_codes, 2) == 1)[:, None, None, None]
    negated = (orient_codes >= 2)[:, None, None, None]
    turned = jnp.where(flipped, jnp.swapaxes(tile_set, 1, 3), tile_set)
    return jnp.where(negated, -turned, turned)


def assemble(tile_set, blocks):
    tile_width = tile_set.shape[1]
    col_tiles = KC // tile_width
    row_tiles = tile_set.shape[0] // col_tiles
    tile_grid = tile_set.reshape(row_tiles, col_tiles, tile_width, blocks, tile_width)
    return tile_grid.transpose(0, 2, 3, 1, 4).reshape(
        row_tiles * tile_width, blocks * col_tiles * tile_width
    )


def antisymmetrize(product):
    height = product.shape[0]
    breadth = product.shape[1]
    blocked = product.reshape(height // VW, VW, breadth // VW, VW)
    return (blocked - blocked.transpose(0, 3, 2, 1)).reshape(height, breadth).astype(jnp.bfloat16)


def on_device(packed_tiles, source_pick, owner_place, tile_orient, w_panel):
    stored = packed_tiles.shape[0]
    tile_width = packed_tiles.shape[1]
    row_peers = lax.axis_size("row")
    peer_slots = stored // row_peers
    blocks = lax.axis_size("col")
    whole_tiles = lax.all_gather(packed_tiles, "col", axis=2, tiled=True)
    outgoing = jnp.take(whole_tiles, source_pick[0], axis=0)
    outgoing = outgoing.reshape(row_peers, peer_slots, tile_width, blocks * tile_width)
    incoming = lax.all_to_all(outgoing, "row", split_axis=0, concat_axis=0, tiled=True)
    incoming = incoming.reshape(stored, tile_width, blocks * tile_width)
    owner_tiles = jnp.take(incoming, owner_place[0], axis=0).reshape(
        stored, tile_width, blocks, tile_width
    )
    lambda_rows = assemble(orient_tiles(owner_tiles, tile_orient[0]), blocks)
    product = jnp.dot(
        lambda_rows,
        lax.all_gather(w_panel, "row", axis=0, tiled=True),
        preferred_element_type=jnp.float32,
    )
    return antisymmetrize(product)


def solution(mesh):
    in_specs = (
        P("row", None, "col"),
        P("row", None),
        P("row", None),
        P("row", None),
        P("row", "col"),
    )
    out_specs = P("row", "col")
    return jax.shard_map(
        on_device, mesh=mesh, in_specs=in_specs, out_specs=out_specs, check_vma=False
    )
```

profile of v0, /device:TPU:33, one launch (start us, length us, event | category | flops | bytes accessed | tf_op | source)
XLA Modules:
  0.0 523.9 jit_solution(2093930135659324942)
XLA Ops:
  6.5 0.7 all-gather.3.cloned.1.call-update
  7.3 0.7 all-gather.5.cloned.1.call-update
  8.0 0.7 compare_select_fusion.1
  8.7 0.7 compare_and_fusion.1
  9.3 134.3 %all-gather.3.cloned.1.call-done = bf16[48,128,1024]{2,1,0:T(8,128)(2,1)} async-done(((bf16[48,128,128]{2,1,0:T(8,128)(2,1)}), bf16[48,128,1024]{2,1,0:T(8,128)(2,1)}) %all-gather.3.cloned.1.call-update) | async-done | bytes 12582928 | tf_op jit(solution)/shard_map/all_gather | solution.py:40
  143.6 10.8 %gather_fusion = bf16[48,128,1024]{2,1,0:T(8,128)(2,1)} fusion(bf16[48,128,1024]{2,1,0:T(8,128)(2,1)} %all-gather.3.cloned.1.call-done, s32[1024]{0:T(1024)S(1)} %pad_clamp_fusion.1), kind=kCustom, calls=%fused_computation.clone | custom fusion | bytes 25166016 | tf_op jit(solution)/shard_map/jit(_take)/gather | solution.py:41
  154.5 10.8 %broadcast_select_fusion.1 = bf16[48,128,1024]{2,1,0:T(8,128)(2,1)} fusion(bf16[48,128,1024]{2,1,0:T(8,128)(2,1)} %gather_fusion, pred[48]{0:T(512)(128)(4,1)S(1)} %compare_and_fusion.1), kind=kLoop, calls=%fused_computation.8 | loop fusion | flops 6291456 | bytes 25165872 | tf_op jit(solution)/shard_map/jit(_take)/select_n | solution.py:41
  165.3 10.7 %all-to-all-start = ((bf16[16,3,128,1024]{3,2,1,0:T(8,128)(2,1)}), bf16[16,3,128,1024]{3,2,1,0:T(8,128)(2,1)}, u32[]{:S(2)}, u32[]{:S(2)}) async-start(bf16[16,3,128,1024]{3,2,1,0:T(8,128)(2,1)} %bitcast.45), calls=%async_computation | async-start | bytes 25165824 | tf_op jit(solution)/shard_map/all_to_all | solution.py:43
  176.1 166.8 %all-gather.5.cloned.1.call-done = bf16[4096,1536]{1,0:T(8,128)(2,1)} async-done(((bf16[256,1536]{1,0:T(8,128)(2,1)}), bf16[4096,1536]{1,0:T(8,128)(2,1)}) %all-gather.5.cloned.1.call-update) | async-done | bytes 12582928 | tf_op jit(solution)/shard_map/all_gather | solution.py:51
  342.8 16.7 %copy.15 = bf16[1536,4096]{1,0:T(8,128)(2,1)} copy(bf16[1536,4096]{0,1:T(8,128)(2,1)} %bitcast.49) | data formatting | bytes 25165824 | tf_op jit(solution)/shard_map/dot_general | solution.py:49
  359.6 10.8 %gather_fusion.1 = bf16[48,128,1024]{2,1,0:T(8,128)(2,1)} fusion(bf16[48,128,1024]{2,1,0:T(8,128)(2,1)} %bitcast.4, s32[1024]{0:T(1024)S(1)} %pad_clamp_fusion), kind=kCustom, calls=%fused_computation.1.clone | custom fusion | bytes 25166016 | tf_op jit(solution)/shard_map/jit(_take)/gather | solution.py:45
  370.4 6.5 %broadcast_select_fusion = bf16[48,128,1024]{2,1,0:T(8,128)(2,1)S(1)} fusion(bf16[48,128,1024]{2,1,0:T(8,128)(2,1)} %gather_fusion.1, pred[48]{0:T(512)(128)(4,1)S(1)} %compare_and_fusion), kind=kLoop, calls=%fused_computation.7 | loop fusion | flops 6291456 | bytes 25165872 | tf_op jit(solution)/shard_map/jit(_take)/select_n | solution.py:45
  376.9 2.9 copy.19
  379.8 4.5 copy-done
  384.3 5.0 bitcast_bitcast_fusion
  389.3 17.9 %copy.13 = bf16[48,128,8,128]{3,2,1,0:T(8,128)(2,1)} copy(bf16[48,128,8,128]{1,2,3,0:T(8,128)(2,1)} %bitcast_bitcast_fusion) | data formatting | bytes 25165824 | tf_op jit(solution)/shard_map/transpose | solution.py:13
  407.2 9.3 %negate_select_fusion = bf16[48,128,8,128]{3,2,1,0:T(8,128)(2,1)S(1)} fusion(bf16[48,128,8,128]{3,2,1,0:T(8,128)(2,1)} %copy.13, pred[48]{0:T(512)(128)(4,1)S(1)} %get-tuple-element.7, pred[48]{0:T(512)(128)(4,1)S(1)} %get-tuple-element.6, bf16[48,128,8,128]{3,2,1,0:T(8,128)(2,1)} %bitcast.44), kind=kLoop, calls=%fused_computation.2 | loop fusion | flops 18874368 | bytes 37748832 | tf_op jit(solution)/shard_map/jit(_where)/select_n | solution.py:14
  416.5 17.1 %copy.14 = bf16[12,128,8,4,128]{4,3,2,1,0:T(4,128)(2,1)} copy(bf16[12,128,8,4,128]{4,2,1,3,0:T(8,128)(2,1)S(1)} %bitcast.46) | data formatting | bytes 25165824 | tf_op jit(solution)/shard_map/transpose | solution.py:22
  433.6 21.1 %reshape.77 = bf16[2,768,4096,1]{2,1,0,3:T(8,128)(2,1)} reshape(bf16[12,128,8,4,128]{4,3,2,1,0:T(4,128)(2,1)} %copy.14) | data formatting | bytes 25165824 | tf_op jit(solution)/shard_map/dot_general | solution.py:49
  454.7 27.9 %fusion = f32[2,768,2,768]{3,1,2,0:T(8,128)} fusion(bf16[2,768,4096,1]{2,1,0,3:T(8,128)(2,1)} %bitcast.50, bf16[2,768,4096,1]{2,1,0,3:T(8,128)(2,1)} %reshape.77), kind=kOutput, calls=%fused_computation.5 | convolution fusion | flops 19327352832 | bytes 34603008 | tf_op jit(solution)/shard_map/dot_general | solution.py:49
  482.6 9.7 %copy.16 = f32[2,768,2,768]{1,3,2,0:T(8,128)} copy(f32[2,768,2,768]{3,1,2,0:T(8,128)} %fusion) | data formatting | bytes 18874368 | tf_op jit(solution)/shard_map/dot_general | solution.py:49
  492.2 10.0 %fusion.2 = bf16[2,768,2,768]{3,1,2,0:T(8,128)(2,1)} fusion(f32[2,768,2,768]{3,1,2,0:T(8,128)} %fusion, f32[2,768,2,768]{1,3,2,0:T(8,128)} %copy.16), kind=kLoop, calls=%fused_computation.10 | loop fusion | flops 4718592 | bytes 23592960 | tf_op jit(solution)/shard_map/convert_element_type | solution.py:31
  502.3 9.3 %copy.17 = bf16[2,768,2,768]{3,2,1,0:T(2,128)(2,1)} copy(bf16[2,768,2,768]{3,1,2,0:T(8,128)(2,1)} %fusion.2) | data formatting | bytes 9437184 | tf_op jit(solution)/shard_map/convert_element_type | solution.py:31
  511.6 5.5 %copy.20 = bf16[192,8,2,768]{3,1,2,0:T(8,128)(2,1)} copy(bf16[192,8,2,768]{3,2,1,0:T(2,128)(2,1)} %bitcast.48) | data formatting | bytes 9437184
  (13 shorter events, 0.1 us)
Async XLA Ops:
  6.5 137.1 %all-gather.3.cloned.1.call-start = ((), (), s32[]{:S(2)}) async-start(), calls=%async_computation.1 | async-start | bytes 14155776 | tf_op jit(solution)/shard_map/all_gather | solution.py:40
  7.3 335.6 %all-gather.5.cloned.1.call-start = ((), (), s32[]{:S(2)}) async-start(), calls=%async_computation.2 | async-start | bytes 13369344 | tf_op jit(solution)/shard_map/all_gather | solution.py:51
  165.3 10.7 %copy-start.1 = (s32[1,48]{1,0:T(1,128)S(1)}, s32[1,48]{1,0:T(1,128)}, u32[]{:S(2)}) copy-start(s32[1,48]{1,0:T(1,128)} %param.9) | copy-start | bytes 580
  165.3 10.8 %copy-start.2 = (s32[1,48]{1,0:T(1,128)S(1)}, s32[1,48]{1,0:T(1,128)}, u32[]{:S(2)}) copy-start(s32[1,48]{1,0:T(1,128)} %param.10) | copy-start | bytes 580
  165.3 194.3 %all-to-all-start = ((bf16[16,3,128,1024]{3,2,1,0:T(8,128)(2,1)}), bf16[16,3,128,1024]{3,2,1,0:T(8,128)(2,1)}, u32[]{:S(2)}, u32[]{:S(2)}) async-start(bf16[16,3,128,1024]{3,2,1,0:T(8,128)(2,1)} %bitcast.45), calls=%async_computation | async-start | bytes 25165824 | tf_op jit(solution)/shard_map/all_to_all | solution.py:43
  379.8 4.5 copy-start
Sparse Core Ops, SparseCore 0:
  8.9 134.6 all-gather.2
  146.1 196.7 all-gather.4
where the time goes:
time: 526 us; the launch traced here: 524 us
  waiting for transfers between devices  302 us (57%)
  local copies, waits for them, and re-layouts  131 us (25%)
  other arithmetic  38.1 us (7%)
  matrix products  27.9 us (5%)
  between operations  13.5 us (3%)
  starting transfers between devices  10.8 us (2%)
    all_gather x1, waiting for transfers between devices, on_device(): lax.all_gather(w_panel, 'row', axis=0, tiled=True)  167 us
    all_gather x1, waiting for transfers between devices, on_device(): whole_tiles = lax.all_gather(packed_tiles, 'col', axis=2, tiled=True)  134 us
    dot_general x3, local copies, waits for them, and re-layouts, on_device(): jnp.dot(lambda_rows, lax.all_gather(w_panel, 'row', axis=0, tiled=True),...  47.5 us
    dot_general x1, matrix products, on_device(): jnp.dot(lambda_rows, lax.all_gather(w_panel, 'row', axis=0, tiled=True),...  27.9 us
    transpose x2, local copies, waits for them, and re-layouts, orient_tiles(): turned = jnp.where(flipped, jnp.swapaxes(tile_set, 1, 3), tile_set)  22.9 us
    transpose x1, local copies, waits for them, and re-layouts, assemble(): tile_grid.transpose(0, 2, 3, 1, 4)  17.1 us
    unnamed x8, local copies, waits for them, and re-layouts  12.8 us
    select_n x2, other arithmetic, on_device(): outgoing = jnp.take(whole_tiles, source_pick[0], axis=0)  11.5 us
  transfers between devices with their start and end apart: 3, of which 2 were waited for; matrix products, arithmetic and copies ran while one was open for 8% of the time, Pallas kernels for 0%

commit v1 on v0

--- a/solution.py
+++ b/solution.py
@@ -48,7 +48,9 @@
     lambda_rows = assemble(orient_tiles(owner_tiles, tile_orient[0]), blocks)
     product = jnp.dot(
         lambda_rows,
-        lax.all_gather(w_panel, "row", axis=0, tiled=True),
+        jnp.concatenate(
+            lax.all_to_all(jnp.stack([w_panel] * lax.axis_size("row")), "row", 0, 0), axis=0
+        ),
         preferred_element_type=jnp.float32,
     )
     return antisymmetrize(product)

time: 526 us -> 595 us (1.13)
  waiting for transfers between devices: 302 us -> 342 us
  local copies, waits for them, and re-layouts: 131 us -> 154 us
    all_gather x1 -> x0, waiting for transfers between devices: 167 us -> none  [on_device(): lax.all_gather(w_panel, 'row', axis=0, tiled=True)]
    all_to_all x0 -> x1, waiting for transfers between devices: none -> 114 us  [on_device(): lax.all_to_all(jnp.stack([w_panel] * lax.axis_size('row')), 'row', 0, 0)]
    all_to_all x1, waiting for transfers between devices: 0.01 us -> 107 us  [on_device(): lax.all_to_all(outgoing, 'row', split_axis=0, concat_axis=0, tiled=True)]
    all_to_all x0 -> x1, local copies, waits for them, and re-layouts: none -> 16 us  [on_device(): lax.all_to_all(jnp.stack([w_panel] * lax.axis_size('row')), 'row', 0, 0)]
    all_gather x1, waiting for transfers between devices: 134 us -> 121 us  [on_device(): whole_tiles = lax.all_gather(packed_tiles, 'col', axis=2, tiled=True)]
    all_to_all x0 -> x1, starting transfers between devices: none -> 8.48 us  [on_device(): lax.all_to_all(jnp.stack([w_panel] * lax.axis_size('row')), 'row', 0, 0)]
    unnamed x8 -> x11, local copies, waits for them, and re-layouts: 12.8 us -> 14.2 us
  transfers between devices with their start and end apart: 3 -> 3, of which waited for: 2 -> 3; matrix products, arithmetic and copies ran while one was open for 8% -> 10% of each run, Pallas kernels for 0% -> 0%
where the time goes in v1:
time: 595 us; the launch traced here: 590 us
  waiting for transfers between devices  342 us (57%)
  local copies, waits for them, and re-layouts  154 us (26%)
  other arithmetic  36.6 us (6%)
  matrix products  27.9 us (5%)
  starting transfers between devices  15.5 us (3%)
  between operations  13.5 us (2%)
    all_gather x1, waiting for transfers between devices, on_device(): whole_tiles = lax.all_gather(packed_tiles, 'col', axis=2, tiled=True)  121 us
    all_to_all x1, waiting for transfers between devices, on_device(): lax.all_to_all(jnp.stack([w_panel] * lax.axis_size('row')), 'row', 0, 0)  114 us
    all_to_all x1, waiting for transfers between devices, on_device(): lax.all_to_all(outgoing, 'row', split_axis=0, concat_axis=0, tiled=True)  107 us
    dot_general x3, local copies, waits for them, and re-layouts, on_device(): jnp.dot(lambda_rows, jnp.concatenate(lax.all_to_all(jnp.stack([w_panel] *...  47.5 us
    dot_general x1, matrix products, on_device(): jnp.dot(lambda_rows, jnp.concatenate(lax.all_to_all(jnp.stack([w_panel] *...  27.9 us
    transpose x2, local copies, waits for them, and re-layouts, orient_tiles(): turned = jnp.where(flipped, jnp.swapaxes(tile_set, 1, 3), tile_set)  22.9 us
    transpose x1, local copies, waits for them, and re-layouts, assemble(): tile_grid.transpose(0, 2, 3, 1, 4)  17.1 us
    all_to_all x1, local copies, waits for them, and re-layouts, on_device(): lax.all_to_all(jnp.stack([w_panel] * lax.axis_size('row')), 'row', 0, 0)  16 us
  transfers between devices with their start and end apart: 3, of which 3 were waited for; matrix products, arithmetic and copies ran while one was open for 10% of the time, Pallas kernels for 0%

profile of v1, /device:TPU:33, one launch (start us, length us, event | category | flops | bytes accessed | tf_op | source)
XLA Modules:
  0.0 590.0 jit_solution(7021249298388788624)
XLA Ops:
  8.7 5.7 stack.2
  14.3 8.5 %all-to-all-start.1 = ((bf16[16,256,1536]{1,2,0:T(8,128)(2,1)}), bf16[16,256,1536]{1,2,0:T(8,128)(2,1)}, u32[]{:S(2)}, u32[]{:S(2)}) async-start(bf16[16,256,1536]{1,2,0:T(8,128)(2,1)} %stack.2), calls=%async_computation.1 | async-start | bytes 25165824 | tf_op jit(solution)/shard_map/all_to_all | solution.py:52
  22.9 120.6 %all-gather.2.cloned.1.call-done = bf16[48,128,1024]{2,1,0:T(8,128)(2,1)} async-done(((bf16[48,128,128]{2,1,0:T(8,128)(2,1)}), bf16[48,128,1024]{2,1,0:T(8,128)(2,1)}) %all-gather.2.cloned.1.call-update) | async-done | bytes 12582928 | tf_op jit(solution)/shard_map/all_gather | solution.py:40
  143.5 10.8 %gather_fusion = bf16[48,128,1024]{2,1,0:T(8,128)(2,1)} fusion(bf16[48,128,1024]{2,1,0:T(8,128)(2,1)} %all-gather.2.cloned.1.call-done, s32[1024]{0:T(1024)S(1)} %pad_clamp_fusion.1), kind=kCustom, calls=%fused_computation.clone | custom fusion | bytes 25166016 | tf_op jit(solution)/shard_map/jit(_take)/gather | solution.py:41
  154.3 10.7 %broadcast_select_fusion.1 = bf16[48,128,1024]{2,1,0:T(8,128)(2,1)} fusion(bf16[48,128,1024]{2,1,0:T(8,128)(2,1)} %gather_fusion, pred[48]{0:T(512)(128)(4,1)S(1)} %compare_and_fusion.1), kind=kLoop, calls=%fused_computation.8 | loop fusion | flops 6291456 | bytes 25165872 | tf_op jit(solution)/shard_map/jit(_take)/select_n | solution.py:41
  165.0 113.9 %all-to-all-done.1 = bf16[16,256,1536]{1,2,0:T(8,128)(2,1)} async-done(((bf16[16,256,1536]{1,2,0:T(8,128)(2,1)}), bf16[16,256,1536]{1,2,0:T(8,128)(2,1)}, u32[]{:S(2)}, u32[]{:S(2)}) %all-to-all-start.1) | async-done | bytes 12582944 | tf_op jit(solution)/shard_map/all_to_all | solution.py:52
  279.0 7.0 %all-to-all-start = ((bf16[16,3,128,1024]{3,2,1,0:T(8,128)(2,1)}), bf16[16,3,128,1024]{3,2,1,0:T(8,128)(2,1)}, u32[]{:S(2)}, u32[]{:S(2)}) async-start(bf16[16,3,128,1024]{3,2,1,0:T(8,128)(2,1)} %bitcast.48), calls=%async_computation | async-start | bytes 25165824 | tf_op jit(solution)/shard_map/all_to_all | solution.py:43
  286.0 16.0 %copy.26 = bf16[16,256,1536]{2,1,0:T(8,128)(2,1)} copy(bf16[16,256,1536]{1,2,0:T(8,128)(2,1)} %all-to-all-done.1) | data formatting | bytes 25165824 | tf_op jit(solution)/shard_map/all_to_all | solution.py:52
  302.0 16.7 %copy.27 = bf16[1536,4096]{1,0:T(8,128)(2,1)} copy(bf16[1536,4096]{0,1:T(8,128)(2,1)} %bitcast.47) | data formatting | bytes 25165824 | tf_op jit(solution)/shard_map/dot_general | solution.py:49
  318.8 106.8 %all-to-all-done = bf16[16,3,128,1024]{3,2,1,0:T(8,128)(2,1)} async-done(((bf16[16,3,128,1024]{3,2,1,0:T(8,128)(2,1)}), bf16[16,3,128,1024]{3,2,1,0:T(8,128)(2,1)}, u32[]{:S(2)}, u32[]{:S(2)}) %all-to-all-start) | async-done | bytes 12582944 | tf_op jit(solution)/shard_map/all_to_all | solution.py:43
  425.5 11.0 %gather_fusion.1 = bf16[48,128,1024]{2,1,0:T(8,128)(2,1)} fusion(bf16[48,128,1024]{2,1,0:T(8,128)(2,1)} %bitcast.4, s32[1024]{0:T(1024)S(1)} %pad_clamp_fusion), kind=kCustom, calls=%fused_computation.1.clone | custom fusion | bytes 25166016 | tf_op jit(solution)/shard_map/jit(_take)/gather | solution.py:45
  436.5 6.5 %broadcast_select_fusion = bf16[48,128,1024]{2,1,0:T(8,128)(2,1)S(1)} fusion(bf16[48,128,1024]{2,1,0:T(8,128)(2,1)} %gather_fusion.1, pred[48]{0:T(512)(128)(4,1)S(1)} %compare_and_fusion), kind=kLoop, calls=%fused_computation.7 | loop fusion | flops 6291456 | bytes 25165872 | tf_op jit(solution)/shard_map/jit(_take)/select_n | solution.py:45
  443.0 2.9 copy.31
  445.9 4.5 copy-done
  450.4 5.0 bitcast_bitcast_fusion
  455.4 17.9 %copy.23 = bf16[48,128,8,128]{3,2,1,0:T(8,128)(2,1)} copy(bf16[48,128,8,128]{1,2,3,0:T(8,128)(2,1)} %bitcast_bitcast_fusion) | data formatting | bytes 25165824 | tf_op jit(solution)/shard_map/transpose | solution.py:13
  473.2 9.3 %negate_select_fusion = bf16[48,128,8,128]{3,2,1,0:T(8,128)(2,1)S(1)} fusion(bf16[48,128,8,128]{3,2,1,0:T(8,128)(2,1)} %copy.23, pred[48]{0:T(512)(128)(4,1)S(1)} %get-tuple-element.7, pred[48]{0:T(512)(128)(4,1)S(1)} %get-tuple-element.6, bf16[48,128,8,128]{3,2,1,0:T(8,128)(2,1)} %bitcast.46), kind=kLoop, calls=%fused_computation.2 | loop fusion | flops 18874368 | bytes 37748832 | tf_op jit(solution)/shard_map/jit(_where)/select_n | solution.py:14
  482.6 17.1 %copy.24 = bf16[12,128,8,4,128]{4,3,2,1,0:T(4,128)(2,1)} copy(bf16[12,128,8,4,128]{4,2,1,3,0:T(8,128)(2,1)S(1)} %bitcast.49) | data formatting | bytes 25165824 | tf_op jit(solution)/shard_map/transpose | solution.py:22
  499.6 21.1 %reshape.83 = bf16[2,768,4096,1]{2,1,0,3:T(8,128)(2,1)} reshape(bf16[12,128,8,4,128]{4,3,2,1,0:T(4,128)(2,1)} %copy.24) | data formatting | bytes 25165824 | tf_op jit(solution)/shard_map/dot_general | solution.py:49
  520.8 27.9 %fusion = f32[2,768,2,768]{3,1,2,0:T(8,128)} fusion(bf16[2,768,4096,1]{2,1,0,3:T(8,128)(2,1)} %bitcast.52, bf16[2,768,4096,1]{2,1,0,3:T(8,128)(2,1)} %reshape.83), kind=kOutput, calls=%fused_computation.5 | convolution fusion | flops 19327352832 | bytes 34603008 | tf_op jit(solution)/shard_map/dot_general | solution.py:49
  548.6 9.7 %copy.28 = f32[2,768,2,768]{1,3,2,0:T(8,128)} copy(f32[2,768,2,768]{3,1,2,0:T(8,128)} %fusion) | data formatting | bytes 18874368 | tf_op jit(solution)/shard_map/dot_general | solution.py:49
  558.3 10.0 %fusion.2 = bf16[2,768,2,768]{3,1,2,0:T(8,128)(2,1)} fusion(f32[2,768,2,768]{3,1,2,0:T(8,128)} %fusion, f32[2,768,2,768]{1,3,2,0:T(8,128)} %copy.28), kind=kLoop, calls=%fused_computation.10 | loop fusion | flops 4718592 | bytes 23592960 | tf_op jit(solution)/shard_map/convert_element_type | solution.py:31
  568.3 9.3 %copy.29 = bf16[2,768,2,768]{3,2,1,0:T(2,128)(2,1)} copy(bf16[2,768,2,768]{3,1,2,0:T(8,128)(2,1)} %fusion.2) | data formatting | bytes 9437184 | tf_op jit(solution)/shard_map/convert_element_type | solution.py:31
  577.7 5.5 copy.32
  (17 shorter events, 2.2 us)
Async XLA Ops:
  6.5 136.9 %all-gather.2.cloned.1.call-start = ((), (), s32[]{:S(2)}) async-start(), calls=%async_computation.2 | async-start | bytes 14155776 | tf_op jit(solution)/shard_map/all_gather | solution.py:40
  14.3 8.5 %copy-start.1 = (s32[1,48]{1,0:T(1,128)S(1)}, s32[1,48]{1,0:T(1,128)}, u32[]{:S(2)}) copy-start(s32[1,48]{1,0:T(1,128)} %param.8) | copy-start | bytes 580
  14.3 264.6 %all-to-all-start.1 = ((bf16[16,256,1536]{1,2,0:T(8,128)(2,1)}), bf16[16,256,1536]{1,2,0:T(8,128)(2,1)}, u32[]{:S(2)}, u32[]{:S(2)}) async-start(bf16[16,256,1536]{1,2,0:T(8,128)(2,1)} %stack.2), calls=%async_computation.1 | async-start | bytes 25165824 | tf_op jit(solution)/shard_map/all_to_all | solution.py:52
  279.0 7.0 %copy-start.2 = (s32[1,48]{1,0:T(1,128)S(1)}, s32[1,48]{1,0:T(1,128)}, u32[]{:S(2)}) copy-start(s32[1,48]{1,0:T(1,128)} %param.9) | copy-start | bytes 580
  279.0 7.1 %copy-start.3 = (s32[1,48]{1,0:T(1,128)S(1)}, s32[1,48]{1,0:T(1,128)}, u32[]{:S(2)}) copy-start(s32[1,48]{1,0:T(1,128)} %param.10) | copy-start | bytes 580
  279.0 146.5 %all-to-all-start = ((bf16[16,3,128,1024]{3,2,1,0:T(8,128)(2,1)}), bf16[16,3,128,1024]{3,2,1,0:T(8,128)(2,1)}, u32[]{:S(2)}, u32[]{:S(2)}) async-start(bf16[16,3,128,1024]{3,2,1,0:T(8,128)(2,1)} %bitcast.48), calls=%async_computation | async-start | bytes 25165824 | tf_op jit(solution)/shard_map/all_to_all | solution.py:43
  445.9 4.5 copy-start
Sparse Core Ops, SparseCore 0:
  8.9 134.5 all-gather.1
